TPU v7x, 512 devices: a whole 4x8x8 slice. The times are simulated.
512 devices in a mesh: dp: 32 (over y_hi, x, core), tensor: 16 (over z, y_lo).
Axes of the slice: x: 4, y: 8 (y_hi: 4, y_lo: 2; y = y_hi * 2 + y_lo), z: 8, core: 2. Of those that a mesh axis runs over, the one named last changes fastest.
Arguments:
- tokens: bfloat16 [12288, 2048], P('dp'), may hold values from -6 to 6
- out_grad: bfloat16 [12288, 7168], P('dp', 'tensor'), may hold values from -6 to 6
- gate_weight: bfloat16 [2048, 7168], P('dp', 'tensor'), may hold values from -0.1875 to 0.1875
- up_weight: bfloat16 [2048, 7168], P('dp', 'tensor'), may hold values from -0.1875 to 0.1875
- gate_mask: int32 [32, 112], P('dp', 'tensor'), may hold values 0 or 1
- up_mask: int32 [32, 112], P('dp', 'tensor'), may hold values 0 or 1
Outputs:
- hidden: float32 [12288, 7168], P('dp', 'tensor')
- grad_tokens: bfloat16 [12288, 2048], P('dp')
- grad_gate: float32 [2048, 7168], P('dp', 'tensor')
- grad_up: float32 [2048, 7168], P('dp', 'tensor')
All inputs are finite; a program needn't handle non-finite values. No bound on the sum of `gate_mask` or of `up_mask` on one device may be relied on, other than what follows from the above.
Results may differ from a plain program's by a relative error of at most 0.014.
Values may be sent and summed in bfloat16 or wider, within the bound.
No kernel may reach another device: no remote copies, remote signals or barrier semaphores. Data moves between devices by JAX's collectives and lax.ppermute only.
A program may use at most 64 MiB of HBM per device.

v0:
```python
import jax
import jax.numpy as jnp
from jax import lax
from jax.sharding import PartitionSpec as P

BLOCK = 64


def expand(block_mask):
    height, breadth = block_mask.shape
    values = block_mask.astype(jnp.float32)
    return jnp.broadcast_to(values[:, None, :, None], (height, BLOCK, breadth, BLOCK)).reshape(
        height * BLOCK, breadth * BLOCK
    )


def local(tokens, out_grad, gate_weight, up_weight, gate_mask, up_mask):
    gate_keep = expand(gate_mask)
    up_keep = expand(up_mask)
    gate_eff = gate_weight * gate_keep.astype(jnp.bfloat16)
    up_eff = up_weight * up_keep.astype(jnp.bfloat16)
    local_both = jnp.concatenate([gate_eff, up_eff], axis=1)
    hidden_width = gate_weight.shape[1]
    gathered = lax.all_gather(local_both, "dp", axis=0, tiled=True)
    preact = jnp.dot(tokens, gathered, preferred_element_type=jnp.float32)
    gate = preact[:, :hidden_width]
    up = preact[:, hidden_width:]
    sigmoid_gate = jax.nn.sigmoid(gate)
    activation = gate * sigmoid_gate
    hidden = activation * up
    grad_float = out_grad.astype(jnp.float32)
    d_gate = (grad_float * up * sigmoid_gate * (1.0 + gate * (1.0 - sigmoid_gate))).astype(
        jnp.bfloat16
    )
    d_up = (grad_float * activation).astype(jnp.bfloat16)
    d_both = jnp.concatenate([d_gate, d_up], axis=1)
    partial_input = lax.dot_general(
        d_both, gathered, (((1,), (1,)), ((), ())), preferred_element_type=jnp.float32
    )
    grad_tokens = lax.psum(partial_input, "tensor").astype(jnp.bfloat16)
    summed = lax.psum_scatter(
        lax.dot_general(
            tokens, d_both, (((0,), (0,)), ((), ())), preferred_element_type=jnp.float32
        ).astype(jnp.bfloat16),
        "dp",
        scatter_dimension=0,
        tiled=True,
    ).astype(jnp.float32)
    grad_gate = summed[:, :hidden_width] * gate_keep
    grad_up = summed[:, hidden_width:] * up_keep
    return (hidden, grad_tokens, grad_gate, grad_up)


def solution(mesh):
    placed = (
        P("dp", None),
        P("dp", "tensor"),
        P("dp", "tensor"),
        P("dp", "tensor"),
        P("dp", "tensor"),
        P("dp", "tensor"),
    )
    return jax.shard_map(
        local,
        mesh=mesh,
        in_specs=placed,
        out_specs=(P("dp", "tensor"), P("dp", None), P("dp", "tensor"), P("dp", "tensor")),
        check_vma=False,
    )
```

profile of v0, /device:TPU:2, one launch (start us, length us, event | category | flops | bytes accessed | tf_op | source)
XLA Modules:
  0.0 270.0 jit_solution(18201012500881110290)
XLA Ops:
  7.2 0.0 copy-start
  7.2 0.0 all-gather.2.cloned.1.call-start
  7.2 0.8 convert_bitcast_fusion.2
  8.0 0.7 convert_bitcast_fusion.1
  8.7 0.1 broadcast_in_dim.33
  8.7 0.1 broadcast_in_dim.34
  8.8 0.1 broadcast_in_dim.29
  8.9 0.1 broadcast_in_dim.30
  9.0 0.9 broadcast_multiply_fusion
  9.9 0.7 pad_maximum_fusion.3
  10.6 0.0 all-gather.2.cloned.1.call-update
  10.6 0.0 copy-start.1
  10.6 0.0 reduce-scatter.4.cloned.1.call-start
  10.7 69.7 %all-gather.2.cloned.1.call-done = bf16[2048,896]{1,0:T(8,128)(2,1)} async-done(((bf16[64,896]{1,0:T(8,128)(2,1)}), bf16[2048,896]{1,0:T(8,128)(2,1)}) %all-gather.2.cloned.1.call-update) | async-done | bytes 3670032 | tf_op jit(solution)/shard_map/all_gather | solution.py:24
  80.3 0.0 copy-done
  80.3 4.1 %convolution_bitcast_fusion = f32[384,896]{0,1:T(8,128)S(1)} fusion(bf16[2048,896]{1,0:T(8,128)(2,1)} %all-gather.2.cloned.1.call-done, bf16[384,2048]{1,0:T(8,128)(2,1)S(1)} %copy-done), kind=kOutput, calls=%fused_computation.1 | convolution fusion | flops 1409286144 | bytes 6619136 | tf_op jit(solution)/shard_map/dot_general | solution.py:25
  84.5 0.0 copy-done.1
  84.5 1.3 fusion.2
  85.7 4.0 %convert_bitcast_fusion = bf16[2048,896]{0,1:T(8,128)(2,1)} fusion(bf16[384,2048]{1,0:T(8,128)(2,1)S(1)} %copy-done, bf16[384,448]{0,1:T(8,128)(2,1)S(1)} %get-tuple-element.13, bf16[384,448]{0,1:T(8,128)(2,1)S(1)} %get-tuple-element.12), kind=kOutput, calls=%fused_computation | convolution fusion | flops 1412497408 | bytes 5931008 | tf_op jit(solution)/shard_map/dot_general | solution.py:42
  89.7 6.1 %copy.14 = bf16[2048,896]{1,0:T(8,128)(2,1)} copy(bf16[2048,896]{0,1:T(8,128)(2,1)} %convert_bitcast_fusion) | data formatting | bytes 7340032
  95.8 0.0 reduce-scatter.4.cloned.1.call-update
  95.8 5.6 %fusion.5 = f32[384,2048]{1,0:T(8,128)} fusion(bf16[2048,896]{1,0:T(8,128)(2,1)} %all-gather.2.cloned.1.call-done, bf16[384,448]{0,1:T(8,128)(2,1)S(1)} %get-tuple-element.13, bf16[384,448]{0,1:T(8,128)(2,1)S(1)} %get-tuple-element.12), kind=kOutput, calls=%fused_computation.12 | convolution fusion | flops 1410662400 | bytes 7503872 | tf_op jit(solution)/shard_map/dot_general | solution.py:37
  101.4 158.8 %all-reduce.1 = bf16[384,2048]{1,0:T(8,128)(2,1)} all-reduce(f32[384,2048]{1,0:T(8,128)} %fusion.5), channel_id=1, replica_groups=mesh['dp'=32,'tensor'=16] {'tensor'}, use_global_device_ids=true, to_apply=%region_0.0 | all-reduce | flops 786432 | bytes 4718592 | tf_op jit(solution)/shard_map/psum | solution.py:40
  260.3 0.0 reduce-scatter.4.cloned.1.call-done
  260.3 1.1 copy.15
  261.4 0.2 slice_multiply_fusion.1
  261.6 0.8 copy.13
  262.4 0.8 copy.12
  (3 shorter events, 0.0 us)
Async XLA Ops:
  7.2 73.2 %copy-start = (bf16[384,2048]{1,0:T(8,128)(2,1)S(1)}, bf16[384,2048]{1,0:T(8,128)(2,1)}, u32[]{:S(2)}) copy-start(bf16[384,2048]{1,0:T(8,128)(2,1)} %param.6) | copy-start | bytes 4718596
  7.2 73.1 %all-gather.2.cloned.1.call-start = ((), (), s32[]{:S(2)}) async-start(), calls=%async_computation.1 | async-start | bytes 3784704 | tf_op jit(solution)/shard_map/all_gather | solution.py:24
  10.6 73.9 %copy-start.1 = (bf16[384,448]{0,1:T(8,128)(2,1)S(1)}, bf16[384,448]{0,1:T(8,128)(2,1)}, u32[]{:S(2)}) copy-start(bf16[384,448]{0,1:T(8,128)(2,1)} %param.7) | copy-start | bytes 1032196
  10.6 249.7 %reduce-scatter.4.cloned.1.call-start = ((), (), s32[]{:S(2)}) async-start(), calls=%async_computation.2 | async-start | bytes 3784704
Sparse Core Ops, SparseCore 0:
  11.7 68.5 all-gather.1
  96.0 108.4 reduce-scatter.3
where the time goes:
time: 270 us
  blocking collectives  159 us (59%)
  waiting for transfers between devices  69.7 us (26%)
  between operations  14.1 us (5%)
  matrix products  13.7 us (5%)
  local copies, waits for them, and re-layouts  8.99 us (3%)
  other arithmetic  4.54 us (2%)
    psum x1, blocking collectives, local(): grad_tokens = lax.psum(partial_input, 'tensor').astype(jnp.bfloat16)  159 us
    all_gather x1, waiting for transfers between devices, local(): gathered = lax.all_gather(local_both, 'dp', axis=0, tiled=True)  69.7 us
    unnamed x8, local copies, waits for them, and re-layouts  8.7 us
    dot_general x1, matrix products, local(): lax.dot_general(d_both, gathered, (((1,), (1,)), ((), ())), preferred_ele...  5.62 us
  transfers between devices with their start and end apart: 2, of which 1 were waited for; matrix products, arithmetic and copies ran while one was open for 2% of the time, Pallas kernels for 0%

commit v1 on v0

--- a/solution.py
+++ b/solution.py
@@ -21,7 +21,9 @@
     up_eff = up_weight * up_keep.astype(jnp.bfloat16)
     local_both = jnp.concatenate([gate_eff, up_eff], axis=1)
     hidden_width = gate_weight.shape[1]
-    gathered = lax.all_gather(local_both, "dp", axis=0, tiled=True)
+    gathered = jnp.concatenate(
+        lax.all_to_all(jnp.stack([local_both] * lax.axis_size("dp")), "dp", 0, 0), axis=0
+    )
     preact = jnp.dot(tokens, gathered, preferred_element_type=jnp.float32)
     gate = preact[:, :hidden_width]
     up = preact[:, hidden_width:]

time: 270 us -> 297 us (1.10)
  the two profiles are of different devices: /device:TPU:2 before, /device:TPU:16 now
where the time goes in v1:
time: 297 us
  blocking collectives  257 us (87%)
  between operations  14.1 us (5%)
  matrix products  11.7 us (4%)
  local copies, waits for them, and re-layouts  9.52 us (3%)
  other arithmetic  3.88 us (1%)
    psum x1, blocking collectives, local(): grad_tokens = lax.psum(partial_input, 'tensor').astype(jnp.bfloat16)  162 us
    all_to_all x1, blocking collectives, local(): lax.all_to_all(jnp.stack([local_both] * lax.axis_size('dp')), 'dp', 0, 0)  95.1 us
    unnamed x10, local copies, waits for them, and re-layouts  8.71 us
  transfers between devices with their start and end apart: 1, of which 0 were waited for; matrix products, arithmetic and copies ran while one was open for 2% of the time, Pallas kernels for 0%

profile of v1, /device:TPU:16, one launch (start us, length us, event | category | flops | bytes accessed | tf_op | source)
XLA Modules:
  0.0 296.5 jit_solution(5327391517222812875)
XLA Ops:
  7.2 0.0 copy-start
  7.2 0.0 reduce-scatter.4.cloned.1.call-start
  7.2 0.8 convert_bitcast_fusion.2
  8.0 0.7 convert_bitcast_fusion.1
  8.7 0.1 broadcast_in_dim.33
  8.7 0.1 broadcast_in_dim.34
  8.8 0.1 broadcast_in_dim.29
  8.9 0.1 broadcast_in_dim.30
  9.0 0.9 broadcast_multiply_fusion
  9.9 0.1 pad_maximum_fusion.3
  9.9 0.5 stack.2
  10.5 95.1 %all_to_all.5 = bf16[32,64,896]{2,1,0:T(8,128)(2,1)S(1)} all-to-all(bf16[32,64,896]{2,1,0:T(8,128)(2,1)S(1)} %stack.2), channel_id=1, replica_groups=mesh['dp'=32,'tensor'=16] {'dp'}, dimensions={0} | all-to-all | bytes 7340032 | tf_op jit(solution)/shard_map/all_to_all | solution.py:25
  105.6 0.0 copy-start.1
  105.6 0.0 copy-done
  105.6 0.0 copy-start.2
  105.6 2.1 convolution_bitcast_fusion
  107.7 0.0 copy-done.1
  107.7 0.0 copy-done.2
  107.7 1.3 fusion.2
  109.0 4.0 %convert_bitcast_fusion = bf16[2048,896]{0,1:T(8,128)(2,1)} fusion(bf16[384,2048]{1,0:T(8,128)(2,1)S(1)} %copy-done, bf16[384,448]{0,1:T(8,128)(2,1)S(1)} %get-tuple-element.13, bf16[384,448]{0,1:T(8,128)(2,1)S(1)} %get-tuple-element.12), kind=kOutput, calls=%fused_computation | convolution fusion | flops 1412497408 | bytes 5931008 | tf_op jit(solution)/shard_map/dot_general | solution.py:44
  112.9 6.1 %copy.14 = bf16[2048,896]{1,0:T(8,128)(2,1)} copy(bf16[2048,896]{0,1:T(8,128)(2,1)} %convert_bitcast_fusion) | data formatting | bytes 7340032
  119.0 0.0 reduce-scatter.4.cloned.1.call-update
  119.1 5.6 %fusion.5 = f32[384,2048]{1,0:T(8,128)} fusion(bf16[2048,896]{1,0:T(8,128)(2,1)} %bitcast.15, bf16[384,448]{0,1:T(8,128)(2,1)S(1)} %get-tuple-element.13, bf16[384,448]{0,1:T(8,128)(2,1)S(1)} %get-tuple-element.12), kind=kOutput, calls=%fused_computation.12 | convolution fusion | flops 1410662400 | bytes 7503872 | tf_op jit(solution)/shard_map/dot_general | solution.py:39
  124.6 162.2 %all-reduce.1 = bf16[384,2048]{1,0:T(8,128)(2,1)} all-reduce(f32[384,2048]{1,0:T(8,128)} %fusion.5), channel_id=1, replica_groups=mesh['dp'=32,'tensor'=16] {'tensor'}, use_global_device_ids=true, to_apply=%region_0.0 | all-reduce | flops 786432 | bytes 4718592 | tf_op jit(solution)/shard_map/psum | solution.py:42
  286.8 0.0 reduce-scatter.4.cloned.1.call-done
  286.8 1.1 copy.15
  288.0 0.2 slice_multiply_fusion.1
  288.1 0.8 copy.13
  288.9 0.8 copy.12
  (3 shorter events, 0.0 us)
Async XLA Ops:
  7.2 98.4 %copy-start = (bf16[384,2048]{1,0:T(8,128)(2,1)S(1)}, bf16[384,2048]{1,0:T(8,128)(2,1)}, u32[]{:S(2)}) copy-start(bf16[384,2048]{1,0:T(8,128)(2,1)} %param.6) | copy-start | bytes 4718596
  7.2 279.7 %reduce-scatter.4.cloned.1.call-start = ((), (), s32[]{:S(2)}) async-start(), calls=%async_computation.2 | async-start | bytes 3784704
  105.6 2.1 copy-start.1
  105.6 2.1 copy-start.2
Sparse Core Ops, SparseCore 0:
  119.2 109.8 reduce-scatter.3

commit v2 on v0

--- a/solution.py
+++ b/solution.py
@@ -37,7 +37,7 @@
     partial_input = lax.dot_general(
         d_both, gathered, (((1,), (1,)), ((), ())), preferred_element_type=jnp.float32
     )
-    grad_tokens = lax.psum(partial_input, "tensor").astype(jnp.bfloat16)
+    grad_tokens = jnp.sum(lax.all_gather(partial_input, "tensor"), axis=0).astype(jnp.bfloat16)
     summed = lax.psum_scatter(
         lax.dot_general(
             tokens, d_both, (((0,), (0,)), ((), ())), preferred_element_type=jnp.float32

time: 270 us -> 1250 us (4.63)
  the two profiles are of different devices: /device:TPU:2 before, /device:TPU:1 now
where the time goes in v2:
time: 1250 us
  waiting for transfers between devices  1190 us (95%)
  other arithmetic  23.2 us (2%)
  between operations  13.8 us (1%)
  matrix products  13.6 us (1%)
    all_gather x1, waiting for transfers between devices, local(): lax.all_gather(partial_input, 'tensor')  1030 us
    unnamed x4, waiting for transfers between devices  95.4 us
    all_gather x1, waiting for transfers between devices, local(): gathered = lax.all_gather(local_both, 'dp', axis=0, tiled=True)  71 us
  transfers between devices with their start and end apart: 3, of which 3 were waited for; matrix products, arithmetic and copies ran while one was open for 1% of the time, Pallas kernels for 0%

profile of v2, /device:TPU:1, one launch (start us, length us, event | category | flops | bytes accessed | tf_op | source)
XLA Modules:
  0.0 1253.0 jit_solution(8944647205983194445)
XLA Ops:
  7.2 0.0 copy-start
  7.2 0.0 all-gather.4.cloned.1.call-start
  7.2 0.8 convert_bitcast_fusion.2
  8.0 0.7 convert_bitcast_fusion.1
  8.7 0.1 broadcast_in_dim.33
  8.7 0.1 broadcast_in_dim.34
  8.8 0.1 broadcast_in_dim.29
  8.9 0.1 broadcast_in_dim.30
  9.0 0.9 broadcast_multiply_fusion
  9.9 0.7 pad_maximum_fusion.3
  10.6 0.0 all-gather.4.cloned.1.call-update
  10.6 0.0 copy-start.2
  10.6 0.0 reduce-scatter.4.cloned.1.call-start
  10.7 71.0 %all-gather.4.cloned.1.call-done = bf16[2048,896]{1,0:T(8,128)(2,1)} async-done(((bf16[64,896]{1,0:T(8,128)(2,1)}), bf16[2048,896]{1,0:T(8,128)(2,1)}) %all-gather.4.cloned.1.call-update) | async-done | bytes 3670032 | tf_op jit(solution)/shard_map/all_gather | solution.py:24
  81.7 0.0 copy-done
  81.7 4.1 convolution_bitcast_fusion
  85.8 0.0 copy-done.2
  85.8 1.3 fusion.2
  87.1 3.9 convert_bitcast_fusion
  91.0 6.1 copy.14
  97.1 0.0 reduce-scatter.4.cloned.1.call-update
  97.1 0.0 all-gather.6.cloned.1.call-start
  97.2 5.6 fusion.5
  102.7 0.0 all-gather.6.cloned.1.call-update
  102.7 95.3 %reduce-scatter.4.cloned.1.call-done = bf16[64,896]{1,0:T(8,128)(2,1)} async-done(((bf16[2048,896]{1,0:T(8,128)(2,1)}), bf16[64,896]{1,0:T(8,128)(2,1)}) %reduce-scatter.4.cloned.1.call-update) | async-done | bytes 114704
  198.1 1.1 copy.15
  199.2 0.2 slice_multiply_fusion.1
  199.4 0.8 copy.13
  200.1 0.8 copy.12
  200.9 1026.9 %all-gather.6.cloned.1.call-done = f32[6144,2048]{1,0:T(8,128)} async-done(((f32[384,2048]{1,0:T(8,128)}), f32[6144,2048]{1,0:T(8,128)}) %all-gather.6.cloned.1.call-update) | async-done | bytes 50331664 | tf_op jit(solution)/shard_map/all_gather | solution.py:40
  1227.8 18.6 %reduce_sum.9 = bf16[384,2048]{1,0:T(8,128)(2,1)} reduce(f32[16,384,2048]{2,1,0:T(8,128)} %bitcast.14, f32[]{:T(128)} %constant.1.clone.1), dimensions={0}, to_apply=%region_0.0 | reduce | flops 11796480 | bytes 51904516 | tf_op jit(solution)/shard_map/reduce_sum | solution.py:40
  1246.5 0.0 copy-done.1
  (4 shorter events, 0.0 us)
Async XLA Ops:
  7.2 74.5 %copy-start = (bf16[384,2048]{1,0:T(8,128)(2,1)S(1)}, bf16[384,2048]{1,0:T(8,128)(2,1)}, u32[]{:S(2)}) copy-start(bf16[384,2048]{1,0:T(8,128)(2,1)} %param.6) | copy-start | bytes 4718596
  7.2 74.5 %all-gather.4.cloned.1.call-start = ((), (), s32[]{:S(2)}) async-start(), calls=%async_computation.1 | async-start | bytes 3784704 | tf_op jit(solution)/shard_map/all_gather | solution.py:24
  10.6 75.2 %copy-start.2 = (bf16[384,448]{0,1:T(8,128)(2,1)S(1)}, bf16[384,448]{0,1:T(8,128)(2,1)}, u32[]{:S(2)}) copy-start(bf16[384,448]{0,1:T(8,128)(2,1)} %param.7) | copy-start | bytes 1032196
  10.6 187.4 %reduce-scatter.4.cloned.1.call-start = ((), (), s32[]{:S(2)}) async-start(), calls=%async_computation.3 | async-start | bytes 3784704
  97.1 1130.7 %all-gather.6.cloned.1.call-start = ((), (), s32[]{:S(2)}) async-start(), calls=%async_computation.2 | async-start | bytes 53477376 | tf_op jit(solution)/shard_map/all_gather | solution.py:40
  1227.8 18.6 %copy-start.1 = (bf16[384,2048]{1,0:T(8,128)(2,1)S(1)}, bf16[384,2048]{1,0:T(8,128)(2,1)}, u32[]{:S(2)}) copy-start(bf16[384,2048]{1,0:T(8,128)(2,1)} %param.6) | copy-start | bytes 4718596
Sparse Core Ops, SparseCore 0:
  11.7 69.9 all-gather.3
  97.2 100.7 reduce-scatter.3
  200.2 1027.6 all-gather.5
